TPU v7x, 256 devices: a whole 4x4x8 slice. The times are simulated.
256 devices in a mesh: seq: 32 (over y, z_lo, core), head: 8 (over x, z_hi).
Axes of the slice: x: 4, y: 4, z: 8 (z_hi: 2, z_lo: 4; z = z_hi * 4 + z_lo), core: 2. Of those that a mesh axis runs over, the one named last changes fastest.
Arguments:
- tokens: bfloat16 [131072, 1024], P(('seq', 'head')), may hold values from -32 to 32
- w_qkv: bfloat16 [1024, 3072], P('seq'), may hold values from -0.1875 to 0.1875
- w_out: bfloat16 [1024, 1024], P('seq'), may hold values from -0.1875 to 0.1875
- neighbours: int32 [1024, 12], P('seq'), may hold values from 0 to 1023, as said below
Outputs:
- update: bfloat16 [131072, 1024], P(('seq', 'head'))
Inputs may be any that keep to these rules, and one draw needn't show every extreme that they name: Block b has grid coordinates z = b // 16, y = (b // 4) % 4, x = b % 4. Each row lists b itself first, then 11 different blocks among its 26 neighbours at offsets -1, 0, 1 in each coordinate (z taken modulo 1024 // 16, y and x modulo 4).
All inputs are finite; a program needn't handle non-finite values.
Results may differ from a plain program's by a relative error of at most 0.0065.
The roundings to bfloat16 on the way count: a program that leaves them out, or rounds other values in their place, can miss the bound.
Values may be sent and summed in bfloat16 or wider, within the bound.
A program may use at most 64 MiB of HBM per device.

v0:
```python
import math
import jax
import jax.numpy as jnp
from jax import lax
from jax.sharding import PartitionSpec as P

HEADS = 8
HD = 128
BLK = 128
NBR = 12
PB = 16


def padded_2(cells, sides, width):
    for axis, dim in sides:
        count = lax.axis_size(axis)
        head = lax.slice_in_dim(cells, 0, width, axis=dim)
        tail = lax.slice_in_dim(cells, cells.shape[dim] - width, cells.shape[dim], axis=dim)
        cells = jnp.concatenate(
            [
                lax.ppermute(tail, axis, [(i, (i + 1) % count) for i in range(count)]),
                cells,
                lax.ppermute(head, axis, [((i + 1) % count, i) for i in range(count)]),
            ],
            axis=dim,
        )
    return cells


def local(tokens, w_qkv, w_out, neighbours):
    head_count = lax.axis_size("head")
    seq_count = lax.axis_size("seq")
    per_device = HEADS // head_count
    local_rows = tokens.shape[0]
    slab_rows = local_rows * head_count
    full_qkv = lax.all_gather(w_qkv, "seq", axis=0, tiled=True)
    projected = jnp.dot(tokens, full_qkv, preferred_element_type=jnp.float32)
    projected = projected.astype(jnp.bfloat16).reshape(local_rows, 3, HEADS, HD)
    slab = lax.all_to_all(projected, "head", split_axis=2, concat_axis=0, tiled=True)
    queries = slab[:, 0]
    key_value = slab[:, 1:3]
    padded = padded_2(key_value, (("seq", 0),), PB * BLK)
    kv_blocks = padded.reshape(-1, BLK, 2, per_device, HD)
    block_count = neighbours.shape[0]
    first_block = lax.axis_index("seq") * block_count
    local_lists = jnp.mod(neighbours - first_block + PB, block_count * seq_count)
    group_blocks = 4
    scale = 1.0 / math.sqrt(HD)

    def attend(args):
        query_group, list_group = args
        picked = kv_blocks[list_group].reshape(group_blocks, NBR * BLK, 2, per_device, HD)
        keys = picked[:, :, 0]
        values = picked[:, :, 1]
        scores = (
            jnp.einsum("nqhd,nkhd->nhqk", query_group, keys, preferred_element_type=jnp.float32)
            * scale
        )
        largest = jnp.max(scores, axis=-1, keepdims=True)
        expo = jnp.exp(scores - largest)
        probs = (expo / jnp.sum(expo, axis=-1, keepdims=True)).astype(jnp.bfloat16)
        result = jnp.einsum("nhqk,nkhd->nqhd", probs, values, preferred_element_type=jnp.float32)
        return result.astype(jnp.bfloat16)

    grouped_q = queries.reshape(block_count // group_blocks, group_blocks, BLK, per_device, HD)
    grouped_l = local_lists.reshape(block_count // group_blocks, group_blocks, NBR)
    attended = lax.map(attend, (grouped_q, grouped_l)).reshape(slab_rows, per_device, HD)
    returned = lax.all_to_all(attended, "head", split_axis=0, concat_axis=1, tiled=True)
    flat = returned.reshape(local_rows, HEADS * HD)
    full_out = lax.all_gather(w_out, "seq", axis=0, tiled=True)
    update = jnp.dot(flat, full_out, preferred_element_type=jnp.float32)
    return update.astype(jnp.bfloat16)


def solution(mesh):
    return jax.shard_map(
        local,
        mesh=mesh,
        in_specs=(P(("seq", "head"), None), P("seq", None), P("seq", None), P("seq", None)),
        out_specs=P(("seq", "head"), None),
        check_vma=False,
    )
```

profile of v0, /device:TPU:33, one launch (start us, length us, event | category | flops | bytes accessed | tf_op | source)
XLA Modules:
  0.0 384.4 jit_solution(7192390426923187747)
XLA Ops:
  6.5 0.7 all-gather.3.cloned.1.call-update
  7.3 71.2 %all-gather.3.cloned.1.call-done = bf16[1024,3072]{1,0:T(8,128)(2,1)} async-done(((bf16[32,3072]{1,0:T(8,128)(2,1)}), bf16[1024,3072]{1,0:T(8,128)(2,1)}) %all-gather.3.cloned.1.call-update) | async-done | bytes 6291472 | tf_op jit(solution)/shard_map/all_gather | solution.py:36
  78.5 6.4 %fusion.29 = bf16[64,8,24,128]{3,1,2,0:T(8,128)(2,1)S(1)} fusion(bf16[512,1024]{1,0:T(8,128)(2,1)S(1)} %copy-done, bf16[1024,3072]{1,0:T(8,128)(2,1)} %all-gather.3.cloned.1.call-done), kind=kOutput, calls=%fused_computation.27 | convolution fusion | flops 3222798336 | bytes 10485760 | tf_op jit(solution)/shard_map/dot_general | solution.py:37
  84.9 0.9 copy.31
  85.8 0.7 copy.20
  86.5 82.3 %all_to_all.33 = bf16[512,3,8,128]{3,0,1,2:T(8,128)(2,1)S(1)} all-to-all(bf16[512,3,8,128]{3,0,1,2:T(8,128)(2,1)S(1)} %copy.20), channel_id=1, replica_groups=mesh['seq'=32,'head'=8] {'head'}, dimensions={2} | all-to-all | bytes 6291456 | tf_op jit(solution)/shard_map/all_to_all | solution.py:39
  168.8 0.3 copy.21
  169.1 1.6 copy-done.1
  170.8 1.1 fusion.34
  171.9 2.4 collective-permute-start
  174.4 1.7 slice.29
  176.2 2.3 slice.31
  178.5 16.8 %collective-permute-done = bf16[2048,2,1,128]{3,0,1,2:T(8,128)(2,1)} collective-permute-done((bf16[2048,2,1,128]{3,0,1,2:T(8,128)(2,1)}, bf16[2048,2,1,128]{3,0,1,2:T(8,128)(2,1)}, u32[]{:S(2)}, u32[]{:S(2)}) %collective-permute-start) | collective-permute-done | bytes 1048608 | tf_op jit(solution)/shard_map/ppermute | solution.py:21
  195.2 8.9 %collective-permute-done.1 = bf16[2048,2,1,128]{3,0,1,2:T(8,128)(2,1)} collective-permute-done((bf16[2048,2,1,128]{3,0,1,2:T(8,128)(2,1)S(1)}, bf16[2048,2,1,128]{3,0,1,2:T(8,128)(2,1)}, u32[]{:S(2)}, u32[]{:S(2)}) %collective-permute-start.1) | collective-permute-done | bytes 1048608 | tf_op jit(solution)/shard_map/ppermute | solution.py:23
  204.2 1.7 pad_maximum_fusion
  205.9 2.2 copy.22
  208.1 123.6 %while.10 = (s32[]{:T(128)}, bf16[8,4,128,1,128]{4,2,1,0,3:T(8,128)(2,1)S(1)}, s32[8,4,12]{2,1,0:T(4,128)S(1)}, bf16[64,128,2,1,128]{4,1,3,2,0:T(8,128)(2,1)}, bf16[8,4,128,1,128]{4,2,1,3,0:T(8,128)(2,1)}, /*index=5*/s32[]{:T(128)}) while((s32[]{:T(128)}, bf16[8,4,128,1,128]{4,2,1,0,3:T(8,128)(2,1)S(1)}, s32[8,4,12]{2,1,0:T(4,128)S(1)}, ...), condition=%wide.region_3.4_spmd, body=%wide.region_0.3_spmd.sunk | while | flops 609555072 | bytes 18229452 | solution.py:67
  208.2 4.9 %gather_fusion = bf16[48,128,2,128]{3,1,2,0:T(8,128)(2,1)} fusion(bf16[64,128,2,128]{3,1,2,0:T(8,128)(2,1)} %bitcast.87, s32[1024]{0:T(1024)S(1)} %pad_clamp_fusion.2), kind=kCustom, calls=%fused_computation.clone.1 | custom fusion | bytes 6291648 | tf_op jit(solution)/shard_map/while/body/eval_jaxpr/gather | solution.py:52
  213.2 4.0 %copy.35 = bf16[48,128,2,128]{3,1,0,2:T(8,128)(2,1)} copy(bf16[48,128,2,128]{3,1,2,0:T(8,128)(2,1)} %gather_fusion) | data formatting | bytes 6291456 | tf_op jit(solution)/shard_map/while/body/eval_jaxpr/gather | solution.py:52
  217.2 2.6 fusion.45
  219.8 3.7 fusion.46
  223.4 0.1 copy.36
  223.7 4.9 %gather_fusion = bf16[48,128,2,128]{3,1,2,0:T(8,128)(2,1)} fusion(bf16[64,128,2,128]{3,1,2,0:T(8,128)(2,1)} %bitcast.87, s32[1024]{0:T(1024)S(1)} %pad_clamp_fusion.2), kind=kCustom, calls=%fused_computation.clone.1 | custom fusion | bytes 6291648 | tf_op jit(solution)/shard_map/while/body/eval_jaxpr/gather | solution.py:52
  228.7 4.0 %copy.35 = bf16[48,128,2,128]{3,1,0,2:T(8,128)(2,1)} copy(bf16[48,128,2,128]{3,1,2,0:T(8,128)(2,1)} %gather_fusion) | data formatting | bytes 6291456 | tf_op jit(solution)/shard_map/while/body/eval_jaxpr/gather | solution.py:52
  232.7 2.6 fusion.45
  235.2 3.6 fusion.46
  239.2 4.9 %gather_fusion = bf16[48,128,2,128]{3,1,2,0:T(8,128)(2,1)} fusion(bf16[64,128,2,128]{3,1,2,0:T(8,128)(2,1)} %bitcast.87, s32[1024]{0:T(1024)S(1)} %pad_clamp_fusion.2), kind=kCustom, calls=%fused_computation.clone.1 | custom fusion | bytes 6291648 | tf_op jit(solution)/shard_map/while/body/eval_jaxpr/gather | solution.py:52
  244.1 4.0 %copy.35 = bf16[48,128,2,128]{3,1,0,2:T(8,128)(2,1)} copy(bf16[48,128,2,128]{3,1,2,0:T(8,128)(2,1)} %gather_fusion) | data formatting | bytes 6291456 | tf_op jit(solution)/shard_map/while/body/eval_jaxpr/gather | solution.py:52
  248.1 2.6 fusion.45
  250.7 3.6 fusion.46
  254.3 0.1 copy.36
  254.6 4.9 %gather_fusion = bf16[48,128,2,128]{3,1,2,0:T(8,128)(2,1)} fusion(bf16[64,128,2,128]{3,1,2,0:T(8,128)(2,1)} %bitcast.87, s32[1024]{0:T(1024)S(1)} %pad_clamp_fusion.2), kind=kCustom, calls=%fused_computation.clone.1 | custom fusion | bytes 6291648 | tf_op jit(solution)/shard_map/while/body/eval_jaxpr/gather | solution.py:52
  259.5 4.0 %copy.35 = bf16[48,128,2,128]{3,1,0,2:T(8,128)(2,1)} copy(bf16[48,128,2,128]{3,1,2,0:T(8,128)(2,1)} %gather_fusion) | data formatting | bytes 6291456 | tf_op jit(solution)/shard_map/while/body/eval_jaxpr/gather | solution.py:52
  263.6 2.6 fusion.45
  266.1 3.6 fusion.46
  269.8 0.1 copy.36
  270.1 4.9 %gather_fusion = bf16[48,128,2,128]{3,1,2,0:T(8,128)(2,1)} fusion(bf16[64,128,2,128]{3,1,2,0:T(8,128)(2,1)} %bitcast.87, s32[1024]{0:T(1024)S(1)} %pad_clamp_fusion.2), kind=kCustom, calls=%fused_computation.clone.1 | custom fusion | bytes 6291648 | tf_op jit(solution)/shard_map/while/body/eval_jaxpr/gather | solution.py:52
  275.0 4.0 %copy.35 = bf16[48,128,2,128]{3,1,0,2:T(8,128)(2,1)} copy(bf16[48,128,2,128]{3,1,2,0:T(8,128)(2,1)} %gather_fusion) | data formatting | bytes 6291456 | tf_op jit(solution)/shard_map/while/body/eval_jaxpr/gather | solution.py:52
  279.0 2.6 fusion.45
  281.6 3.6 fusion.46
  285.2 0.1 copy.36
  285.5 4.9 %gather_fusion = bf16[48,128,2,128]{3,1,2,0:T(8,128)(2,1)} fusion(bf16[64,128,2,128]{3,1,2,0:T(8,128)(2,1)} %bitcast.87, s32[1024]{0:T(1024)S(1)} %pad_clamp_fusion.2), kind=kCustom, calls=%fused_computation.clone.1 | custom fusion | bytes 6291648 | tf_op jit(solution)/shard_map/while/body/eval_jaxpr/gather | solution.py:52
  290.4 4.0 %copy.35 = bf16[48,128,2,128]{3,1,0,2:T(8,128)(2,1)} copy(bf16[48,128,2,128]{3,1,2,0:T(8,128)(2,1)} %gather_fusion) | data formatting | bytes 6291456 | tf_op jit(solution)/shard_map/while/body/eval_jaxpr/gather | solution.py:52
  294.4 2.6 fusion.45
  297.0 3.6 fusion.46
  300.7 0.1 copy.36
  300.9 4.9 %gather_fusion = bf16[48,128,2,128]{3,1,2,0:T(8,128)(2,1)} fusion(bf16[64,128,2,128]{3,1,2,0:T(8,128)(2,1)} %bitcast.87, s32[1024]{0:T(1024)S(1)} %pad_clamp_fusion.2), kind=kCustom, calls=%fused_computation.clone.1 | custom fusion | bytes 6291648 | tf_op jit(solution)/shard_map/while/body/eval_jaxpr/gather | solution.py:52
  305.9 4.0 %copy.35 = bf16[48,128,2,128]{3,1,0,2:T(8,128)(2,1)} copy(bf16[48,128,2,128]{3,1,2,0:T(8,128)(2,1)} %gather_fusion) | data formatting | bytes 6291456 | tf_op jit(solution)/shard_map/while/body/eval_jaxpr/gather | solution.py:52
  309.9 2.6 fusion.45
  312.5 3.6 fusion.46
  316.1 0.1 copy.36
  316.4 4.9 %gather_fusion = bf16[48,128,2,128]{3,1,2,0:T(8,128)(2,1)} fusion(bf16[64,128,2,128]{3,1,2,0:T(8,128)(2,1)} %bitcast.87, s32[1024]{0:T(1024)S(1)} %pad_clamp_fusion.2), kind=kCustom, calls=%fused_computation.clone.1 | custom fusion | bytes 6291648 | tf_op jit(solution)/shard_map/while/body/eval_jaxpr/gather | solution.py:52
  321.3 4.0 %copy.35 = bf16[48,128,2,128]{3,1,0,2:T(8,128)(2,1)} copy(bf16[48,128,2,128]{3,1,2,0:T(8,128)(2,1)} %gather_fusion) | data formatting | bytes 6291456 | tf_op jit(solution)/shard_map/while/body/eval_jaxpr/gather | solution.py:52
  325.3 2.6 fusion.45
  327.9 3.6 fusion.46
  331.5 0.1 copy.36
  331.7 0.5 broadcast.55
  332.2 1.4 reduce.4
  333.7 0.3 reshape.97
  334.0 32.8 %all_to_all.34 = bf16[8,2,32768]{2,1,0:T(2,128)(2,1)} all-to-all(bf16[8,2,32768]{2,1,0:T(2,128)(2,1)S(1)} %reshape.97), channel_id=1, replica_groups=mesh['seq'=32,'head'=8] {'head'}, dimensions={0} | all-to-all | bytes 2097152 | tf_op jit(solution)/shard_map/all_to_all | solution.py:68
  366.8 4.3 %reshape.98 = bf16[4096,1,128]{2,1,0:T(2,128)(2,1)S(1)} reshape(bf16[8,2,32768]{2,1,0:T(2,128)(2,1)} %all_to_all.34) | data formatting | bytes 2097152
  371.1 1.1 copy.30
  372.2 1.5 copy.26
  373.7 3.8 convolution_convert_fusion.1
  (46 shorter events, 1.3 us)
Async XLA Ops:
  6.5 71.9 %copy-start = (bf16[512,1024]{1,0:T(8,128)(2,1)S(1)}, bf16[512,1024]{1,0:T(8,128)(2,1)}, u32[]{:S(2)}) copy-start(bf16[512,1024]{1,0:T(8,128)(2,1)} %param.6) | copy-start | bytes 3145732
  6.5 71.9 %all-gather.3.cloned.1.call-start = ((), (), s32[]{:S(2)}) async-start(), calls=%async_computation.2 | async-start | bytes 6488064 | tf_op jit(solution)/shard_map/all_gather | solution.py:36
  7.3 366.5 %all-gather.5.cloned.1.call-start = ((), (), s32[]{:S(2)}) async-start(), calls=%async_computation.3 | async-start | bytes 2162688 | tf_op jit(solution)/shard_map/all_gather | solution.py:70
  169.1 1.7 copy-start.1
  169.1 5.2 %copy-start.2 = (s32[32,12]{0,1:T(8,128)S(1)}, s32[32,12]{0,1:T(8,128)}, u32[]{:S(2)}) copy-start(s32[32,12]{0,1:T(8,128)} %param.9) | copy-start | bytes 4612
  171.9 23.4 %collective-permute-start = (bf16[2048,2,1,128]{3,0,1,2:T(8,128)(2,1)}, bf16[2048,2,1,128]{3,0,1,2:T(8,128)(2,1)}, u32[]{:S(2)}, u32[]{:S(2)}) collective-permute-start(bf16[2048,2,1,128]{3,0,1,2:T(8,128)(2,1)} %get-tuple-element.53), channel_id=1, source_target_pairs={{0,8},{8,16},{16,24},{24,32},{32,40},{40,48},{48,56},{56,64},{64,7... | collective-permute-start | bytes 3145736 | tf_op jit(solution)/shard_map/ppermute | solution.py:21
  174.3 29.9 %collective-permute-start.1 = (bf16[2048,2,1,128]{3,0,1,2:T(8,128)(2,1)S(1)}, bf16[2048,2,1,128]{3,0,1,2:T(8,128)(2,1)}, u32[]{:S(2)}, u32[]{:S(2)}) collective-permute-start(bf16[2048,2,1,128]{3,0,1,2:T(8,128)(2,1)S(1)} %get-tuple-element.54), channel_id=1, source_target_pairs={{8,0},{16,8},{24,16},{32,24},{40,32},{48,40},{56,48},{64,56},{72,6... | collective-permute-start | bytes 3145736 | tf_op jit(solution)/shard_map/ppermute | solution.py:23
Sparse Core Ops, SparseCore 0:
  9.2 69.2 all-gather.2
  174.4 60.0 all-gather.4
where the time goes:
time: 386 us; the launch traced here: 384 us
  blocking collectives  115 us (30%)
  waiting for transfers between devices  97.6 us (25%)
  local copies, waits for them, and re-layouts  92.1 us (24%)
  matrix products  59.9 us (16%)
  between operations  13.5 us (3%)
    all_to_all x1, blocking collectives, local(): lax.all_to_all(projected, 'head', split_axis=2, concat_axis=0, tiled=True)  82.3 us
    gather x16, local copies, waits for them, and re-layouts, attend(): kv_blocks[list_group].reshape(group_blocks, NBR * BLK, 2, per_device, HD)  71.6 us
    all_gather x1, waiting for transfers between devices, local(): full_qkv = lax.all_gather(w_qkv, 'seq', axis=0, tiled=True)  71.2 us
    all_to_all x1, blocking collectives, local(): lax.all_to_all(attended, 'head', split_axis=0, concat_axis=1, tiled=True)  32.8 us
    dot_general x8, matrix products, attend(): jnp.einsum('nhqk,nkhd->nqhd', probs, values, preferred_element_type=jnp.f...  29.2 us
    sub x8, matrix products, attend(): expo = jnp.exp(scores - largest)  20.5 us
    ppermute x1, waiting for transfers between devices, padded_2(): lax.ppermute(tail, axis, [(i, (i + 1) % count) for i in range(count)])  16.8 us
    ppermute x1, waiting for transfers between devices, padded_2(): lax.ppermute(head, axis, [((i + 1) % count, i) for i in range(count)])  8.94 us
  transfers between devices with their start and end apart: 4, of which 3 were waited for; matrix products, arithmetic and copies ran while one was open for 37% of the time, Pallas kernels for 0%

commit v1 on v0

--- a/solution.py
+++ b/solution.py
@@ -33,7 +33,9 @@
     per_device = HEADS // head_count
     local_rows = tokens.shape[0]
     slab_rows = local_rows * head_count
-    full_qkv = lax.all_gather(w_qkv, "seq", axis=0, tiled=True)
+    full_qkv = jnp.concatenate(
+        lax.all_to_all(jnp.stack([w_qkv] * lax.axis_size("seq")), "seq", 0, 0), axis=0
+    )
     projected = jnp.dot(tokens, full_qkv, preferred_element_type=jnp.float32)
     projected = projected.astype(jnp.bfloat16).reshape(local_rows, 3, HEADS, HD)
     slab = lax.all_to_all(projected, "head", split_axis=2, concat_axis=0, tiled=True)

time: 386 us -> 453 us (1.17)
  the two profiles are of different devices: /device:TPU:33 before, /device:TPU:48 now
where the time goes in v1:
time: 453 us; the launch traced here: 451 us
  blocking collectives  264 us (58%)
  local copies, waits for them, and re-layouts  94 us (21%)
  matrix products  57.1 us (13%)
  waiting for transfers between devices  17.7 us (4%)
  between operations  13.5 us (3%)
    all_to_all x1, blocking collectives, local(): lax.all_to_all(jnp.stack([w_qkv] * lax.axis_size('seq')), 'seq', 0, 0)  145 us
    all_to_all x1, blocking collectives, local(): lax.all_to_all(projected, 'head', split_axis=2, concat_axis=0, tiled=True)  83.6 us
    gather x16, local copies, waits for them, and re-layouts, attend(): kv_blocks[list_group].reshape(group_blocks, NBR * BLK, 2, per_device, HD)  71.6 us
    all_to_all x1, blocking collectives, local(): lax.all_to_all(attended, 'head', split_axis=0, concat_axis=1, tiled=True)  34.7 us
    dot_general x8, matrix products, attend(): jnp.einsum('nhqk,nkhd->nqhd', probs, values, preferred_element_type=jnp.f...  29.1 us
    sub x8, matrix products, attend(): expo = jnp.exp(scores - largest)  20.5 us
    ppermute x1, waiting for transfers between devices, padded_2(): lax.ppermute(tail, axis, [(i, (i + 1) % count) for i in range(count)])  15.8 us
  transfers between devices with their start and end apart: 3, of which 2 were waited for; matrix products, arithmetic and copies ran while one was open for 31% of the time, Pallas kernels for 0%

profile of v1, /device:TPU:48, one launch (start us, length us, event | category | flops | bytes accessed | tf_op | source)
XLA Modules:
  0.0 451.2 jit_solution(6694071674010428455)
XLA Ops:
  6.5 1.8 stack.2
  8.3 145.2 %all_to_all.38 = bf16[32,32,3072]{2,1,0:T(8,128)(2,1)S(1)} all-to-all(bf16[32,32,3072]{2,1,0:T(8,128)(2,1)S(1)} %stack.2), channel_id=1, replica_groups=mesh['seq'=32,'head'=8] {'seq'}, dimensions={0} | all-to-all | bytes 12582912 | tf_op jit(solution)/shard_map/all_to_all | solution.py:37
  153.6 3.7 fusion.29
  157.2 0.9 copy.31
  158.1 0.7 copy.20
  158.8 83.6 %all_to_all.39 = bf16[512,3,8,128]{3,0,1,2:T(8,128)(2,1)S(1)} all-to-all(bf16[512,3,8,128]{3,0,1,2:T(8,128)(2,1)S(1)} %copy.20), channel_id=1, replica_groups=mesh['seq'=32,'head'=8] {'head'}, dimensions={2} | all-to-all | bytes 6291456 | tf_op jit(solution)/shard_map/all_to_all | solution.py:41
  242.4 0.3 copy.21
  242.7 1.6 copy-done.1
  244.4 1.1 fusion.34
  245.5 1.7 collective-permute-start.1
  247.4 1.7 slice.29
  249.1 2.3 slice.31
  251.5 15.8 %collective-permute-done = bf16[2048,2,1,128]{3,0,1,2:T(8,128)(2,1)} collective-permute-done((bf16[2048,2,1,128]{3,0,1,2:T(8,128)(2,1)}, bf16[2048,2,1,128]{3,0,1,2:T(8,128)(2,1)}, u32[]{:S(2)}, u32[]{:S(2)}) %collective-permute-start) | collective-permute-done | bytes 1048608 | tf_op jit(solution)/shard_map/ppermute | solution.py:21
  267.3 1.8 collective-permute-done.1
  269.1 1.7 pad_maximum_fusion
  270.8 2.2 copy.22
  273.0 123.6 %while.10 = (s32[]{:T(128)}, bf16[8,4,128,1,128]{4,2,1,0,3:T(8,128)(2,1)S(1)}, s32[8,4,12]{2,1,0:T(4,128)S(1)}, bf16[64,128,2,1,128]{4,1,3,2,0:T(8,128)(2,1)}, bf16[8,4,128,1,128]{4,2,1,3,0:T(8,128)(2,1)}, /*index=5*/s32[]{:T(128)}) while((s32[]{:T(128)}, bf16[8,4,128,1,128]{4,2,1,0,3:T(8,128)(2,1)S(1)}, s32[8,4,12]{2,1,0:T(4,128)S(1)}, ...), condition=%wide.region_3.4_spmd, body=%wide.region_0.3_spmd.sunk | while | flops 609555072 | bytes 18229452 | solution.py:69
  273.1 4.9 %gather_fusion = bf16[48,128,2,128]{3,1,2,0:T(8,128)(2,1)} fusion(bf16[64,128,2,128]{3,1,2,0:T(8,128)(2,1)} %bitcast.88, s32[1024]{0:T(1024)S(1)} %pad_clamp_fusion.2), kind=kCustom, calls=%fused_computation.clone.1 | custom fusion | bytes 6291648 | tf_op jit(solution)/shard_map/while/body/eval_jaxpr/gather | solution.py:54
  278.1 4.0 copy.35
  282.1 2.6 fusion.45
  284.7 3.7 fusion.46
  288.3 0.1 copy.36
  288.6 5.0 %gather_fusion = bf16[48,128,2,128]{3,1,2,0:T(8,128)(2,1)} fusion(bf16[64,128,2,128]{3,1,2,0:T(8,128)(2,1)} %bitcast.88, s32[1024]{0:T(1024)S(1)} %pad_clamp_fusion.2), kind=kCustom, calls=%fused_computation.clone.1 | custom fusion | bytes 6291648 | tf_op jit(solution)/shard_map/while/body/eval_jaxpr/gather | solution.py:54
  293.6 4.0 copy.35
  297.6 2.6 fusion.45
  300.2 3.6 fusion.46
  303.8 0.1 copy.36
  304.1 4.9 %gather_fusion = bf16[48,128,2,128]{3,1,2,0:T(8,128)(2,1)} fusion(bf16[64,128,2,128]{3,1,2,0:T(8,128)(2,1)} %bitcast.88, s32[1024]{0:T(1024)S(1)} %pad_clamp_fusion.2), kind=kCustom, calls=%fused_computation.clone.1 | custom fusion | bytes 6291648 | tf_op jit(solution)/shard_map/while/body/eval_jaxpr/gather | solution.py:54
  309.0 4.0 copy.35
  313.1 2.6 fusion.45
  315.6 3.6 fusion.46
  319.3 0.1 copy.36
  319.6 4.9 %gather_fusion = bf16[48,128,2,128]{3,1,2,0:T(8,128)(2,1)} fusion(bf16[64,128,2,128]{3,1,2,0:T(8,128)(2,1)} %bitcast.88, s32[1024]{0:T(1024)S(1)} %pad_clamp_fusion.2), kind=kCustom, calls=%fused_computation.clone.1 | custom fusion | bytes 6291648 | tf_op jit(solution)/shard_map/while/body/eval_jaxpr/gather | solution.py:54
  324.5 4.0 copy.35
  328.5 2.6 fusion.45
  331.1 3.6 fusion.46
  334.7 0.1 copy.36
  335.0 4.9 %gather_fusion = bf16[48,128,2,128]{3,1,2,0:T(8,128)(2,1)} fusion(bf16[64,128,2,128]{3,1,2,0:T(8,128)(2,1)} %bitcast.88, s32[1024]{0:T(1024)S(1)} %pad_clamp_fusion.2), kind=kCustom, calls=%fused_computation.clone.1 | custom fusion | bytes 6291648 | tf_op jit(solution)/shard_map/while/body/eval_jaxpr/gather | solution.py:54
  339.9 4.0 copy.35
  344.0 2.6 fusion.45
  346.5 3.6 fusion.46
  350.2 0.1 copy.36
  350.5 4.9 %gather_fusion = bf16[48,128,2,128]{3,1,2,0:T(8,128)(2,1)} fusion(bf16[64,128,2,128]{3,1,2,0:T(8,128)(2,1)} %bitcast.88, s32[1024]{0:T(1024)S(1)} %pad_clamp_fusion.2), kind=kCustom, calls=%fused_computation.clone.1 | custom fusion | bytes 6291648 | tf_op jit(solution)/shard_map/while/body/eval_jaxpr/gather | solution.py:54
  355.4 4.0 copy.35
  359.4 2.6 fusion.45
  362.0 3.6 fusion.46
  365.6 0.1 copy.36
  365.9 4.9 %gather_fusion = bf16[48,128,2,128]{3,1,2,0:T(8,128)(2,1)} fusion(bf16[64,128,2,128]{3,1,2,0:T(8,128)(2,1)} %bitcast.88, s32[1024]{0:T(1024)S(1)} %pad_clamp_fusion.2), kind=kCustom, calls=%fused_computation.clone.1 | custom fusion | bytes 6291648 | tf_op jit(solution)/shard_map/while/body/eval_jaxpr/gather | solution.py:54
  370.8 4.0 copy.35
  374.9 2.6 fusion.45
  377.4 3.6 fusion.46
  381.1 0.1 copy.36
  381.4 4.9 %gather_fusion = bf16[48,128,2,128]{3,1,2,0:T(8,128)(2,1)} fusion(bf16[64,128,2,128]{3,1,2,0:T(8,128)(2,1)} %bitcast.88, s32[1024]{0:T(1024)S(1)} %pad_clamp_fusion.2), kind=kCustom, calls=%fused_computation.clone.1 | custom fusion | bytes 6291648 | tf_op jit(solution)/shard_map/while/body/eval_jaxpr/gather | solution.py:54
  386.3 4.0 copy.35
  390.3 2.6 fusion.45
  392.9 3.6 fusion.46
  396.7 0.5 broadcast.57
  397.2 1.4 reduce.4
  398.6 0.3 reshape.103
  398.9 34.7 %all_to_all.40 = bf16[8,2,32768]{2,1,0:T(2,128)(2,1)} all-to-all(bf16[8,2,32768]{2,1,0:T(2,128)(2,1)S(1)} %reshape.103), channel_id=1, replica_groups=mesh['seq'=32,'head'=8] {'head'}, dimensions={0} | all-to-all | bytes 2097152 | tf_op jit(solution)/shard_map/all_to_all | solution.py:70
  433.6 4.3 reshape.104
  437.9 1.1 copy.30
  439.1 1.5 copy.26
  440.6 3.8 convolution_convert_fusion.1
  (45 shorter events, 1.3 us)
Async XLA Ops:
  6.5 147.0 %copy-start = (bf16[512,1024]{1,0:T(8,128)(2,1)S(1)}, bf16[512,1024]{1,0:T(8,128)(2,1)}, u32[]{:S(2)}) copy-start(bf16[512,1024]{1,0:T(8,128)(2,1)} %param.6) | copy-start | bytes 3145732
  6.5 434.0 %all-gather.2.cloned.1.call-start = ((), (), s32[]{:S(2)}) async-start(), calls=%async_computation.3 | async-start | bytes 2162688 | tf_op jit(solution)/shard_map/all_gather | solution.py:72
  242.7 1.7 copy-start.1
  242.7 4.6 %copy-start.2 = (s32[32,12]{0,1:T(8,128)S(1)}, s32[32,12]{0,1:T(8,128)}, u32[]{:S(2)}) copy-start(s32[32,12]{0,1:T(8,128)} %param.9) | copy-start | bytes 4612
  245.5 21.8 %collective-permute-start = (bf16[2048,2,1,128]{3,0,1,2:T(8,128)(2,1)}, bf16[2048,2,1,128]{3,0,1,2:T(8,128)(2,1)}, u32[]{:S(2)}, u32[]{:S(2)}) collective-permute-start(bf16[2048,2,1,128]{3,0,1,2:T(8,128)(2,1)} %get-tuple-element.53), channel_id=1, source_target_pairs={{0,8},{8,16},{16,24},{24,32},{32,40},{40,48},{48,56},{56,64},{64,7... | collective-permute-start | bytes 3145736 | tf_op jit(solution)/shard_map/ppermute | solution.py:21
  245.5 23.6 %collective-permute-start.1 = (bf16[2048,2,1,128]{3,0,1,2:T(8,128)(2,1)S(1)}, bf16[2048,2,1,128]{3,0,1,2:T(8,128)(2,1)}, u32[]{:S(2)}, u32[]{:S(2)}) collective-permute-start(bf16[2048,2,1,128]{3,0,1,2:T(8,128)(2,1)S(1)} %get-tuple-element.54), channel_id=1, source_target_pairs={{8,0},{16,8},{24,16},{32,24},{40,32},{48,40},{56,48},{64,56},{72,6... | collective-permute-start | bytes 3145736 | tf_op jit(solution)/shard_map/ppermute | solution.py:23
Sparse Core Ops, SparseCore 0:
  247.4 62.1 all-gather.1
